TPU v7x, 512 devices: a whole 4x4x16 slice. The times are simulated.
512 devices in a mesh: tm: 8 (over y, core), chan: 64 (over z, x).
Axes of the slice: x: 4, y: 4, z: 16, core: 2. Of those that a mesh axis runs over, the one named last changes fastest.
Arguments:
- spectra: bfloat16 [8, 8192, 8192], P('tm', 'chan'), may hold values from -6 to 6
- block_counts: int32 [64], replicated, may hold values from 1 to 128, 6144 in all
- pairs: int32 [96, 3], replicated, may hold values from 0 to 63, as said below
Outputs:
- stacks: float32 [192, 128, 1024], P('chan', 'tm')
Inputs may be any that keep to these rules, and one draw needn't show every extreme that they name: `pairs`: each owner holds at most 3 pair blocks and some owner holds exactly 3; all pair blocks of one owner share their source block; a target block never equals its source block.
All inputs are finite; a program needn't handle non-finite values.
Results may differ from a plain program's by a relative error of at most 0.0049.
Values may be sent and summed in bfloat16 or wider, within the bound.
A program may use at most 128 MiB of HBM per device.

v0:
```python
import math
import jax
import jax.numpy as jnp
from jax import lax
from jax.sharding import PartitionSpec as P

F = 4096
BAND = 64
LAGS = 8
SLOTS = 3


def phase_tables():
    freq_index = (
        jnp.arange(F // BAND, dtype=jnp.int32)[:, None] * BAND
        + jnp.arange(BAND, dtype=jnp.int32)[None, :]
    )
    lag_values = jnp.arange(LAGS, dtype=jnp.int32) - LAGS // 2
    phase = jnp.mod(lag_values[:, None, None] * freq_index[None], 2 * F)
    angle = jnp.pi * phase.astype(jnp.float32) / F
    return (jnp.cos(angle), jnp.sin(angle))


def whiten(raw, live_count):
    segs, rows, width = raw.shape
    values = raw.astype(jnp.float32).reshape(segs, rows, width // (2 * BAND), 2, BAND)
    power = jnp.mean(values[..., 0, :] ** 2 + values[..., 1, :] ** 2, axis=-1)
    alive = (jnp.arange(rows, dtype=jnp.int32) < live_count).astype(jnp.float32)
    scaled = values * lax.rsqrt(power + 1e-06)[..., None, None] * alive[None, :, None, None, None]
    return scaled.astype(jnp.bfloat16).reshape(segs, rows, width)


def correlate(source, target, cosine, sine, scale):
    groups, segs, rows, width = source.shape
    bands = width // (2 * BAND)
    src = source.reshape(groups, segs, rows, bands, 2, BAND)
    tgt = (
        target.reshape(groups, segs, rows, bands, 2, BAND)
        .transpose(1, 2, 0, 3, 4, 5)
        .astype(jnp.float32)
    )
    real_part = tgt[..., 0, :][:, None]
    imag_part = tgt[..., 1, :][:, None]
    cos_b = cosine.reshape(LAGS, groups, bands, BAND)[None, :, None]
    sin_b = sine.reshape(LAGS, groups, bands, BAND)[None, :, None]
    mod_real = real_part * cos_b + imag_part * sin_b
    mod_imag = imag_part * cos_b - real_part * sin_b
    moved = jnp.stack([mod_real, mod_imag], axis=-2).astype(jnp.bfloat16)
    corr = jnp.einsum("ksiqpf,smjkqpf->imj", src, moved, preferred_element_type=jnp.float32)
    return (corr * scale).reshape(rows, LAGS * rows)


def per_device(spectra, block_counts, pairs):
    chan_count = lax.axis_size("chan")
    my_index = lax.axis_index("chan")
    segs, rows, width = spectra.shape
    scale = 1.0 / math.sqrt(2.0 * F * segs * lax.axis_size("tm"))
    cosine, sine = phase_tables()
    device_ids = jnp.arange(chan_count, dtype=jnp.int32)
    live_count = jnp.sum(jnp.where(device_ids == my_index, block_counts, 0))
    whitened = whiten(spectra, live_count)
    held = lax.all_to_all(whitened[None], "chan", split_axis=3, concat_axis=0, tiled=True)
    owners = pairs[:, 2]
    places = jnp.arange(pairs.shape[0], dtype=jnp.int32)
    earlier = (owners[:, None] == owners[None, :]) & (places[None, :] < places[:, None])
    ranks = jnp.sum(earlier.astype(jnp.int32), axis=1)
    slot_ids = jnp.arange(SLOTS, dtype=jnp.int32)
    matches = (
        (owners[None, None, :] == device_ids[:, None, None])
        & (ranks[None, None, :] == slot_ids[None, :, None])
    ).astype(jnp.int32)
    source_table = jnp.sum(matches * pairs[:, 0][None, None, :], axis=2)
    target_table = jnp.sum(matches * pairs[:, 1][None, None, :], axis=2)
    valid_table = jnp.sum(matches, axis=2)
    my_valid = jnp.sum(jnp.where(device_ids[:, None] == my_index, valid_table, 0), axis=0).astype(
        jnp.float32
    )
    send_source = jnp.take(held, source_table, axis=0)
    send_target = jnp.take(held, target_table, axis=0)
    src_all = lax.all_to_all(send_source, "chan", split_axis=0, concat_axis=0, tiled=True)
    tgt_all = lax.all_to_all(send_target, "chan", split_axis=0, concat_axis=0, tiled=True)

    def one_item(position):
        src_one = lax.dynamic_index_in_dim(src_all, position, 1, False)
        tgt_one = lax.dynamic_index_in_dim(tgt_all, position, 1, False)
        return correlate(src_one, tgt_one, cosine, sine, scale)

    results = lax.map(one_item, jnp.arange(src_all.shape[1], dtype=jnp.int32))
    results = results * my_valid[:, None, None]
    return lax.psum_scatter(results, "tm", scatter_dimension=1, tiled=True)


def solution(mesh):
    placed = (P("tm", "chan", None), P(), P())
    return jax.shard_map(
        per_device, mesh=mesh, in_specs=placed, out_specs=P("chan", "tm", None), check_vma=False
    )
```

profile of v0, /device:TPU:2, one launch (start us, length us, event | category | flops | bytes accessed | tf_op | source)
XLA Modules:
  0.0 956.7 jit_solution(11877595196581559371)
XLA Ops:
  6.5 3.2 copy.33
  10.3 0.6 fusion.23
  10.9 0.6 select_reduce_fusion.1
  11.5 0.6 compare_convert_fusion
  12.8 33.3 %copy.53 = bf16[1,1,128,8192]{2,1,0,3:T(2,128)(2,1)} copy(bf16[1,1,128,8192]{2,3,1,0:T(8,128)(2,1)S(1)} %fusion.21) | data formatting | bytes 4194304 | tf_op jit(solution)/shard_map/convert_element_type | solution.py:30
  46.5 45.2 %reduce.2 = bf16[8192,128]{1,0:T(8,128)(2,1)S(1)} reduce(bf16[8192,1,1,128]{3,2,1,0:T(2,128)(2,1)} %bitcast.78, bf16[]{:T(256)} %broadcast.250), dimensions={1,2}, to_apply=%bitcast.55.reduce_sub_computation | reduce | bytes 4194306
  91.7 2.1 reshape.305
  93.8 18.8 %all-to-all-start = ((bf16[64,2,8192]{2,1,0:T(2,128)(2,1)}), bf16[64,2,8192]{2,1,0:T(2,128)(2,1)S(1)}, u32[]{:S(2)}, u32[]{:S(2)}) async-start(bf16[64,2,8192]{2,1,0:T(2,128)(2,1)} %reshape.305), calls=%async_computation | async-start | bytes 4194304 | tf_op jit(solution)/shard_map/all_to_all | solution.py:62
  113.5 99.2 %all-to-all-done = bf16[64,2,8192]{2,1,0:T(2,128)(2,1)S(1)} async-done(((bf16[64,2,8192]{2,1,0:T(2,128)(2,1)}), bf16[64,2,8192]{2,1,0:T(2,128)(2,1)S(1)}, u32[]{:S(2)}, u32[]{:S(2)}) %all-to-all-start) | async-done | bytes 2097184 | tf_op jit(solution)/shard_map/all_to_all | solution.py:62
  212.8 6.8 reshape.306
  219.5 3.8 copy.50
  223.3 3.2 copy.35
  226.5 8.0 gather_fusion
  234.5 8.6 copy.37
  243.2 6.1 broadcast_select_fusion
  249.3 6.1 all-to-all-start.1
  255.7 7.9 gather_fusion.1
  263.7 6.0 select_bitcast_fusion
  269.7 265.0 %all-to-all-done.1 = bf16[64,3,1,128,128]{3,4,2,1,0:T(8,128)(2,1)} async-done(((bf16[64,3,1,128,128]{3,4,2,1,0:T(8,128)(2,1)}), bf16[64,3,1,128,128]{3,4,2,1,0:T(8,128)(2,1)}, u32[]{:S(2)}, u32[]{:S(2)}) %all-to-all-start.1) | async-done | bytes 6291488 | tf_op jit(solution)/shard_map/all_to_all | solution.py:80
  534.7 6.1 all-to-all-start.2
  541.3 0.7 iota_add_fusion
  542.0 278.2 %all-to-all-done.2 = bf16[64,3,1,128,128]{4,3,1,2,0:T(8,128)(2,1)} async-done(((bf16[64,3,1,128,128]{4,3,1,2,0:T(8,128)(2,1)}), bf16[64,3,1,128,128]{4,3,1,2,0:T(8,128)(2,1)}, u32[]{:S(2)}, u32[]{:S(2)}) %all-to-all-start.2) | async-done | bytes 6291488 | tf_op jit(solution)/shard_map/all_to_all | solution.py:81
  820.2 94.2 %while.13 = (s32[]{:T(128)}, f32[3,128,1024]{2,1,0:T(8,128)}, s32[3]{0:T(128)S(1)}, bf16[64,3,1,128,128]{3,4,2,1,0:T(8,128)(2,1)}, bf16[64,3,1,128,128]{4,3,1,2,...) while((s32[]{:T(128)}, f32[3,128,1024]{2,1,0:T(8,128)}, ...), condition=%wide.region_6.8_spmd.clone.clone.clone, body=%wide.region_5.7_spmd.clone.clone.clone.sunk | while | flops 2216230912 | bytes 70271672 | solution.py:88
  820.2 0.6 dynamic_slice.27
  822.6 3.2 constant_dynamic-slice_fusion.5
  825.8 3.2 copy.56
  829.9 1.9 fusion.35
  831.7 9.9 %add_convert_fusion.2 = (bf16[8,128,64,1,64]{1,4,3,0,2:T(8,128)(2,1)S(1)}, bf16[8,128,64,1,64]{1,4,3,0,2:T(8,128)(2,1)S(1)}) fusion(f32[8,64,64]{2,0,1:T(8,128)S(1)} %get-tuple-element.231, f32[128,64,64]{0,2,1:T(8,128)S(1)} %get-tuple-element.232, f32[8,64,64]{2,0,1:T(8,128)S(1)} %get-tuple-element.233, f32[128,64,64]{0,2,1:T(8,128)S(1)} %get-tuple-element.234), kind=kLoop, calls=%fused_computation.9.clone.1 | loop fusion | flops 33554432 | bytes 21233664 | tf_op jit(solution)/shard_map/convert.2
  841.6 1.7 constant_dynamic-slice_fusion.4
  843.4 7.1 fusion.36
  850.7 0.8 constant_dynamic-update-slice_fusion.2
  851.6 0.6 dynamic_slice.27
  854.0 3.2 constant_dynamic-slice_fusion.5
  857.2 3.2 copy.56
  861.3 1.9 fusion.35
  863.1 9.9 %add_convert_fusion.2 = (bf16[8,128,64,1,64]{1,4,3,0,2:T(8,128)(2,1)S(1)}, bf16[8,128,64,1,64]{1,4,3,0,2:T(8,128)(2,1)S(1)}) fusion(f32[8,64,64]{2,0,1:T(8,128)S(1)} %get-tuple-element.231, f32[128,64,64]{0,2,1:T(8,128)S(1)} %get-tuple-element.232, f32[8,64,64]{2,0,1:T(8,128)S(1)} %get-tuple-element.233, f32[128,64,64]{0,2,1:T(8,128)S(1)} %get-tuple-element.234), kind=kLoop, calls=%fused_computation.9.clone.1 | loop fusion | flops 33554432 | bytes 21233664 | tf_op jit(solution)/shard_map/convert.2
  873.1 1.7 constant_dynamic-slice_fusion.4
  874.8 7.1 fusion.36
  882.2 0.9 constant_dynamic-update-slice_fusion.2
  885.4 3.2 constant_dynamic-slice_fusion.5
  888.7 3.2 copy.56
  892.7 1.9 fusion.35
  894.6 9.9 %add_convert_fusion.2 = (bf16[8,128,64,1,64]{1,4,3,0,2:T(8,128)(2,1)S(1)}, bf16[8,128,64,1,64]{1,4,3,0,2:T(8,128)(2,1)S(1)}) fusion(f32[8,64,64]{2,0,1:T(8,128)S(1)} %get-tuple-element.231, f32[128,64,64]{0,2,1:T(8,128)S(1)} %get-tuple-element.232, f32[8,64,64]{2,0,1:T(8,128)S(1)} %get-tuple-element.233, f32[128,64,64]{0,2,1:T(8,128)S(1)} %get-tuple-element.234), kind=kLoop, calls=%fused_computation.9.clone.1 | loop fusion | flops 33554432 | bytes 21233664 | tf_op jit(solution)/shard_map/convert.2
  904.5 1.7 constant_dynamic-slice_fusion.4
  906.2 7.1 fusion.36
  913.6 0.8 constant_dynamic-update-slice_fusion.2
  914.4 2.9 broadcast_multiply_fusion
  917.3 32.6 %reduce-scatter.2.cloned.1.call-done = f32[3,16,1024]{2,1,0:T(8,128)} async-done(((f32[3,128,1024]{2,1,0:T(8,128)}), f32[3,16,1024]{2,1,0:T(8,128)}) %reduce-scatter.2.cloned.1.call-update) | async-done | bytes 196624 | tf_op jit(solution)/shard_map/reduce_scatter | solution.py:90
  (42 shorter events, 6.8 us)
Async XLA Ops:
  9.8 1.1 copy-start.1
  91.7 20.9 %copy-start = (s32[96,3]{0,1:T(4,128)S(1)}, s32[96,3]{0,1:T(4,128)}, u32[]{:S(2)}) copy-start(s32[96,3]{0,1:T(4,128)} %param.9) | copy-start | bytes 3460
  93.8 118.9 %all-to-all-start = ((bf16[64,2,8192]{2,1,0:T(2,128)(2,1)}), bf16[64,2,8192]{2,1,0:T(2,128)(2,1)S(1)}, u32[]{:S(2)}, u32[]{:S(2)}) async-start(bf16[64,2,8192]{2,1,0:T(2,128)(2,1)} %reshape.305), calls=%async_computation | async-start | bytes 4194304 | tf_op jit(solution)/shard_map/all_to_all | solution.py:62
  249.3 285.5 %all-to-all-start.1 = ((bf16[64,3,1,128,128]{3,4,2,1,0:T(8,128)(2,1)}), bf16[64,3,1,128,128]{3,4,2,1,0:T(8,128)(2,1)}, u32[]{:S(2)}, u32[]{:S(2)}) async-start(bf16[64,3,1,128,128]{3,4,2,1,0:T(8,128)(2,1)} %broadcast_select_fusion), calls=%async_computation.1 | async-start | bytes 12582912 | tf_op jit(solution)/shard_map/all_to_all | solution.py:80
  534.7 285.4 %all-to-all-start.2 = ((bf16[64,3,1,128,128]{4,3,1,2,0:T(8,128)(2,1)}), bf16[64,3,1,128,128]{4,3,1,2,0:T(8,128)(2,1)}, u32[]{:S(2)}, u32[]{:S(2)}) async-start(bf16[64,3,1,128,128]{4,3,1,2,0:T(8,128)(2,1)} %select_bitcast_fusion), calls=%async_computation.2 | async-start | bytes 12582912 | tf_op jit(solution)/shard_map/all_to_all | solution.py:81
  540.8 409.1 %reduce-scatter.2.cloned.1.call-start = ((), (), s32[]{:S(2)}) async-start(), calls=%async_computation.4 | async-start | bytes 1769472 | tf_op jit(solution)/shard_map/reduce_scatter | solution.py:90
Sparse Core Ops, SparseCore 0:
  917.4 32.4 reduce-scatter.1
where the time goes:
time: 958 us; the launch traced here: 957 us
  waiting for transfers between devices  675 us (70%)
  local copies, waits for them, and re-layouts  109 us (11%)
  other arithmetic  101 us (11%)
  starting transfers between devices  31.3 us (3%)
  matrix products  21.4 us (2%)
  between operations  13.6 us (1%)
    all_to_all x1, waiting for transfers between devices, per_device(): lax.all_to_all(send_target, 'chan', split_axis=0, concat_axis=0, tiled=True)  278 us
    all_to_all x1, waiting for transfers between devices, per_device(): lax.all_to_all(send_source, 'chan', split_axis=0, concat_axis=0, tiled=True)  265 us
    all_to_all x1, waiting for transfers between devices, per_device(): lax.all_to_all(whitened[None], 'chan', split_axis=3, concat_axis=0, tiled...  99.2 us
    unnamed x1, other arithmetic  45.2 us
    convert_element_type x1, local copies, waits for them, and re-layouts, whiten(): return scaled.astype(jnp.bfloat16).reshape(segs, rows, width)  33.3 us
    reduce_scatter x1, waiting for transfers between devices, per_device(): return lax.psum_scatter(results, 'tm', scatter_dimension=1, tiled=True)  32.6 us
    another operation x3, other arithmetic  29.7 us
    dot_general x3, matrix products, correlate(): jnp.einsum('ksiqpf,smjkqpf->imj', src, moved, preferred_element_type=jnp....  21.4 us
  transfers between devices with their start and end apart: 4, of which 4 were waited for; matrix products, arithmetic and copies ran while one was open for 2% of the time, Pallas kernels for 0%

commit v1 on v0

--- a/solution.py
+++ b/solution.py
@@ -59,7 +59,12 @@
     device_ids = jnp.arange(chan_count, dtype=jnp.int32)
     live_count = jnp.sum(jnp.where(device_ids == my_index, block_counts, 0))
     whitened = whiten(spectra, live_count)
-    held = lax.all_to_all(whitened[None], "chan", split_axis=3, concat_axis=0, tiled=True)
+    held = jnp.concatenate(
+        lax.all_to_all(
+            jnp.stack(jnp.split(whitened[None], lax.axis_size("chan"), 3), 0), "chan", 0, 0
+        ),
+        0,
+    )
     owners = pairs[:, 2]
     places = jnp.arange(pairs.shape[0], dtype=jnp.int32)
     earlier = (owners[:, None] == owners[None, :]) & (places[None, :] < places[:, None])

time: 958 us -> 900 us (0.939)
  other arithmetic: 101 us -> 53.1 us
  local copies, waits for them, and re-layouts: 109 us -> 97.7 us
    unnamed x1 -> x0, other arithmetic: 45.2 us -> none
    convert_element_type x1 -> x0, local copies, waits for them, and re-layouts: 33.3 us -> none  [whiten(): return scaled.astype(jnp.bfloat16).reshape(segs, rows, width)]
    unnamed x9 -> x68, local copies, waits for them, and re-layouts: 16.4 us -> 41.3 us
    all_to_all x1, waiting for transfers between devices: 265 us -> 279 us  [per_device(): lax.all_to_all(send_source, 'chan', split_axis=0, concat_axis=0, tiled=True)]
    all_to_all x1, waiting for transfers between devices: 278 us -> 265 us  [per_device(): lax.all_to_all(send_target, 'chan', split_axis=0, concat_axis=0, tiled=True)]
where the time goes in v1:
time: 900 us; the launch traced here: 898 us
  waiting for transfers between devices  676 us (75%)
  local copies, waits for them, and re-layouts  97.7 us (11%)
  other arithmetic  53.1 us (6%)
  starting transfers between devices  31 us (3%)
  matrix products  21.4 us (2%)
  between operations  13.6 us (2%)
    all_to_all x1, waiting for transfers between devices, per_device(): lax.all_to_all(send_source, 'chan', split_axis=0, concat_axis=0, tiled=True)  279 us
    all_to_all x1, waiting for transfers between devices, per_device(): lax.all_to_all(send_target, 'chan', split_axis=0, concat_axis=0, tiled=True)  265 us
    all_to_all x1, waiting for transfers between devices, per_device(): lax.all_to_all(jnp.stack(jnp.split(whitened[None], lax.axis_size('chan'),...  99.2 us
    unnamed x68, local copies, waits for them, and re-layouts  41.3 us
    reduce_scatter x1, waiting for transfers between devices, per_device(): return lax.psum_scatter(results, 'tm', scatter_dimension=1, tiled=True)  32.6 us
    another operation x3, other arithmetic  29.7 us
    dot_general x3, matrix products, correlate(): jnp.einsum('ksiqpf,smjkqpf->imj', src, moved, preferred_element_type=jnp....  21.4 us
    dynamic_slice x6, local copies, waits for them, and re-layouts, one_item(): tgt_one = lax.dynamic_index_in_dim(tgt_all, position, 1, False)  19.3 us
  transfers between devices with their start and end apart: 4, of which 4 were waited for; matrix products, arithmetic and copies ran while one was open for 2% of the time, Pallas kernels for 0%

profile of v1, /device:TPU:2, one launch (start us, length us, event | category | flops | bytes accessed | tf_op | source)
XLA Modules:
  0.0 898.4 jit_solution(15878176134808692359)
XLA Ops:
  6.5 3.2 copy.28
  10.3 0.6 fusion.23
  10.9 0.6 select_reduce_fusion.1
  11.5 0.6 compare_convert_fusion
  15.8 0.6 constant_dynamic-update-slice_fusion.59
  18.8 0.6 constant_dynamic-update-slice_fusion.54
  30.9 0.6 constant_dynamic-update-slice_fusion.34
  35.1 0.6 constant_dynamic-update-slice_fusion.27
  36.4 0.6 constant_dynamic-update-slice_fusion.25
  40.0 0.6 constant_dynamic-update-slice_fusion.19
  51.5 18.8 %all-to-all-start = ((bf16[64,1,1,128,128]{3,4,2,1,0:T(8,128)(2,1)}), bf16[64,1,1,128,128]{3,4,2,1,0:T(8,128)(2,1)S(1)}, u32[]{:S(2)}, u32[]{:S(2)}) async-start(bf16[64,1,1,128,128]{3,4,2,1,0:T(8,128)(2,1)} %constant_dynamic-update-slice_fusion.1), calls=%async_computation | async-start | bytes 4194304 | tf_op jit(solution)/shard_map/all_to_all | solution.py:63
  71.1 99.2 %all-to-all-done = bf16[64,1,1,128,128]{3,4,2,1,0:T(8,128)(2,1)S(1)} async-done(((bf16[64,1,1,128,128]{3,4,2,1,0:T(8,128)(2,1)}), bf16[64,1,1,128,128]{3,4,2,1,0:T(8,128)(2,1)S(1)}, u32[]{:S(2)}, u32[]{:S(2)}) %all-to-all-start) | async-done | bytes 2097184 | tf_op jit(solution)/shard_map/all_to_all | solution.py:63
  170.4 8.0 gather_fusion.1
  178.4 8.7 copy.33
  187.0 6.1 select_bitcast_fusion
  193.1 6.1 all-to-all-start.2
  199.6 7.9 gather_fusion
  207.6 6.0 broadcast_select_fusion
  213.6 265.0 %all-to-all-done.2 = bf16[64,3,1,128,128]{4,3,1,2,0:T(8,128)(2,1)} async-done(((bf16[64,3,1,128,128]{4,3,1,2,0:T(8,128)(2,1)}), bf16[64,3,1,128,128]{4,3,1,2,0:T(8,128)(2,1)}, u32[]{:S(2)}, u32[]{:S(2)}) %all-to-all-start.2) | async-done | bytes 6291488 | tf_op jit(solution)/shard_map/all_to_all | solution.py:86
  478.6 6.1 all-to-all-start.1
  485.0 279.1 %all-to-all-done.1 = bf16[64,3,1,128,128]{3,4,2,1,0:T(8,128)(2,1)} async-done(((bf16[64,3,1,128,128]{3,4,2,1,0:T(8,128)(2,1)}), bf16[64,3,1,128,128]{3,4,2,1,0:T(8,128)(2,1)}, u32[]{:S(2)}, u32[]{:S(2)}) %all-to-all-start.1) | async-done | bytes 6291488 | tf_op jit(solution)/shard_map/all_to_all | solution.py:85
  764.0 92.0 %while.13 = (s32[]{:T(128)}, f32[3,128,1024]{2,1,0:T(8,128)}, s32[3]{0:T(128)S(1)}, bf16[64,3,1,128,128]{3,4,2,1,0:T(8,128)(2,1)}, bf16[64,3,1,128,128]{4,3,1,2,...) while((s32[]{:T(128)}, f32[3,128,1024]{2,1,0:T(8,128)}, ...), condition=%wide.region_6.8_spmd.clone.clone.clone, body=%wide.region_5.7_spmd.clone.clone.clone.sunk | while | flops 2216230912 | bytes 70402800 | solution.py:93
  764.0 0.6 dynamic_slice.27
  766.5 3.2 constant_dynamic-slice_fusion.5
  769.7 3.2 copy.47
  773.7 1.1 fusion.35
  774.8 9.9 %add_convert_fusion.2 = (bf16[8,128,64,1,64]{1,4,3,0,2:T(8,128)(2,1)S(1)}, bf16[8,128,64,1,64]{1,4,3,0,2:T(8,128)(2,1)S(1)}) fusion(f32[8,64,64]{2,0,1:T(8,128)S(1)} %get-tuple-element.222, f32[128,64,64]{0,2,1:T(8,128)S(1)} %get-tuple-element.223, f32[8,64,64]{2,0,1:T(8,128)S(1)} %get-tuple-element.224, f32[128,64,64]{0,2,1:T(8,128)S(1)} %get-tuple-element.225), kind=kLoop, calls=%fused_computation.9.clone.1 | loop fusion | flops 33554432 | bytes 21233664 | tf_op jit(solution)/shard_map/convert.2
  784.8 1.7 constant_dynamic-slice_fusion.4
  786.5 7.1 fusion.36
  793.9 0.8 constant_dynamic-update-slice_fusion.66
  794.7 0.6 dynamic_slice.27
  797.1 3.2 constant_dynamic-slice_fusion.5
  800.4 3.2 copy.47
  804.4 1.1 fusion.35
  805.5 9.9 %add_convert_fusion.2 = (bf16[8,128,64,1,64]{1,4,3,0,2:T(8,128)(2,1)S(1)}, bf16[8,128,64,1,64]{1,4,3,0,2:T(8,128)(2,1)S(1)}) fusion(f32[8,64,64]{2,0,1:T(8,128)S(1)} %get-tuple-element.222, f32[128,64,64]{0,2,1:T(8,128)S(1)} %get-tuple-element.223, f32[8,64,64]{2,0,1:T(8,128)S(1)} %get-tuple-element.224, f32[128,64,64]{0,2,1:T(8,128)S(1)} %get-tuple-element.225), kind=kLoop, calls=%fused_computation.9.clone.1 | loop fusion | flops 33554432 | bytes 21233664 | tf_op jit(solution)/shard_map/convert.2
  815.4 1.7 constant_dynamic-slice_fusion.4
  817.2 7.1 fusion.36
  824.5 0.9 constant_dynamic-update-slice_fusion.66
  825.4 0.6 dynamic_slice.27
  827.8 3.2 constant_dynamic-slice_fusion.5
  831.1 3.2 copy.47
  835.1 1.1 fusion.35
  836.2 9.9 %add_convert_fusion.2 = (bf16[8,128,64,1,64]{1,4,3,0,2:T(8,128)(2,1)S(1)}, bf16[8,128,64,1,64]{1,4,3,0,2:T(8,128)(2,1)S(1)}) fusion(f32[8,64,64]{2,0,1:T(8,128)S(1)} %get-tuple-element.222, f32[128,64,64]{0,2,1:T(8,128)S(1)} %get-tuple-element.223, f32[8,64,64]{2,0,1:T(8,128)S(1)} %get-tuple-element.224, f32[128,64,64]{0,2,1:T(8,128)S(1)} %get-tuple-element.225), kind=kLoop, calls=%fused_computation.9.clone.1 | loop fusion | flops 33554432 | bytes 21233664 | tf_op jit(solution)/shard_map/convert.2
  846.1 1.7 constant_dynamic-slice_fusion.4
  847.9 7.1 fusion.36
  855.3 0.8 constant_dynamic-update-slice_fusion.66
  856.1 2.9 broadcast_multiply_fusion
  859.0 32.6 %reduce-scatter.2.cloned.1.call-done = f32[3,16,1024]{2,1,0:T(8,128)} async-done(((f32[3,128,1024]{2,1,0:T(8,128)}), f32[3,16,1024]{2,1,0:T(8,128)}) %reduce-scatter.2.cloned.1.call-update) | async-done | bytes 196624 | tf_op jit(solution)/shard_map/reduce_scatter | solution.py:95
  (112 shorter events, 40.6 us)
Async XLA Ops:
  10.2 0.7 copy-start.3
  51.5 18.8 %copy-start.2 = (s32[96,3]{0,1:T(4,128)S(1)}, s32[96,3]{0,1:T(4,128)}, u32[]{:S(2)}) copy-start(s32[96,3]{0,1:T(4,128)} %param.9) | copy-start | bytes 3460
  51.5 118.9 %all-to-all-start = ((bf16[64,1,1,128,128]{3,4,2,1,0:T(8,128)(2,1)}), bf16[64,1,1,128,128]{3,4,2,1,0:T(8,128)(2,1)S(1)}, u32[]{:S(2)}, u32[]{:S(2)}) async-start(bf16[64,1,1,128,128]{3,4,2,1,0:T(8,128)(2,1)} %constant_dynamic-update-slice_fusion.1), calls=%async_computation | async-start | bytes 4194304 | tf_op jit(solution)/shard_map/all_to_all | solution.py:63
  193.1 285.5 %all-to-all-start.2 = ((bf16[64,3,1,128,128]{4,3,1,2,0:T(8,128)(2,1)}), bf16[64,3,1,128,128]{4,3,1,2,0:T(8,128)(2,1)}, u32[]{:S(2)}, u32[]{:S(2)}) async-start(bf16[64,3,1,128,128]{4,3,1,2,0:T(8,128)(2,1)} %select_bitcast_fusion), calls=%async_computation.2 | async-start | bytes 12582912 | tf_op jit(solution)/shard_map/all_to_all | solution.py:86
  478.6 285.4 %all-to-all-start.1 = ((bf16[64,3,1,128,128]{3,4,2,1,0:T(8,128)(2,1)}), bf16[64,3,1,128,128]{3,4,2,1,0:T(8,128)(2,1)}, u32[]{:S(2)}, u32[]{:S(2)}) async-start(bf16[64,3,1,128,128]{3,4,2,1,0:T(8,128)(2,1)} %broadcast_select_fusion), calls=%async_computation.1 | async-start | bytes 12582912 | tf_op jit(solution)/shard_map/all_to_all | solution.py:85
  484.7 406.9 %reduce-scatter.2.cloned.1.call-start = ((), (), s32[]{:S(2)}) async-start(), calls=%async_computation.4 | async-start | bytes 1769472 | tf_op jit(solution)/shard_map/reduce_scatter | solution.py:95
  764.0 9.7 %copy-start = (s32[64,64]{1,0:T(8,128)}, s32[64,64]{1,0:T(8,128)S(1)}, u32[]{:S(2)}) copy-start(s32[64,64]{1,0:T(8,128)S(1)} %get-tuple-element.253) | copy-start | bytes 49156 | tf_op jit(solution)/shard_map/while
  793.7 1.0 copy-start.1
  794.7 9.7 %copy-start = (s32[64,64]{1,0:T(8,128)}, s32[64,64]{1,0:T(8,128)S(1)}, u32[]{:S(2)}) copy-start(s32[64,64]{1,0:T(8,128)S(1)} %get-tuple-element.253) | copy-start | bytes 49156 | tf_op jit(solution)/shard_map/while
  824.3 1.1 copy-start.1
  825.4 9.7 %copy-start = (s32[64,64]{1,0:T(8,128)}, s32[64,64]{1,0:T(8,128)S(1)}, u32[]{:S(2)}) copy-start(s32[64,64]{1,0:T(8,128)S(1)} %get-tuple-element.253) | copy-start | bytes 49156 | tf_op jit(solution)/shard_map/while
  855.0 1.0 copy-start.1
Sparse Core Ops, SparseCore 0:
  859.1 32.4 reduce-scatter.1
